TPU v7x, 32 devices: a whole 2x2x4 slice. The times are simulated.
32 devices in a mesh: parts: 2 (over x), row: 8 (over z, y), col: 2 (over core).
Axes of the slice: x: 2, y: 2, z: 4, core: 2. Of those that a mesh axis runs over, the one named last changes fastest.
Arguments:
- spectra: bfloat16 [4, 32, 2, 32, 1024], P('parts', None, None, ('row', 'col')), parts along dimension 0, may hold values from -6 to 6
- window_flags: int32 [64, 32], P('parts', ('row', 'col')), parts along dimension 0, may hold values 0 or 1
Outputs:
- cross: float32 [4, 2, 2, 16, 32, 1024], P('parts', None, 'col', None, 'row'), parts along dimension 0
There are 2 independent parts, one for each index of `parts`. A program takes and returns all parts, laid end to end along the dimension named above; each array names one. Nothing has to cross between parts.
All inputs are finite; a program needn't handle non-finite values. No bound on the sum of `window_flags` on one device may be relied on, other than what follows from the above.
Results may differ from a plain program's by a relative error of at most 0.0034.
Values may be sent and summed in bfloat16 or wider, within the bound.
A program may use at most 256 MiB of HBM per device.

v0:
```python
import jax
import jax.numpy as jnp
from jax import lax
from jax.sharding import PartitionSpec as P

HALFWIN = 64
epsilon = 1e-06


def window_mean(magnitude):
    bins = magnitude.shape[-1]
    lead = [(0, 0)] * (magnitude.ndim - 1)
    padded = jnp.pad(magnitude, lead + [(HALFWIN + 1, HALFWIN)])
    running = jnp.cumsum(padded, axis=-1)
    total = running[..., 2 * HALFWIN + 1 :] - running[..., :bins]
    positions = jnp.arange(bins, dtype=jnp.int32)
    counted = (
        jnp.minimum(positions + HALFWIN, bins - 1) - jnp.maximum(positions - HALFWIN, 0) + 1
    ).astype(jnp.float32)
    return total / counted


def whiten(values):
    magnitude = jnp.sqrt(values[:, :, 0] * values[:, :, 0] + values[:, :, 1] * values[:, :, 1])
    smooth = window_mean(magnitude)
    return (values / (smooth[:, :, None] + epsilon)).astype(jnp.bfloat16)


def combine_parts(prods, keep):
    real_part = prods[..., 0, 0, :, :, :] + prods[..., 1, 1, :, :, :]
    imag_part = prods[..., 1, 0, :, :, :] - prods[..., 0, 1, :, :, :]
    return jnp.stack([real_part * keep, imag_part * keep], axis=-4)


def on_device(spectra, window_flags):
    per_device = spectra.shape[3]
    flag_values = window_flags.astype(jnp.float32)[None, :, None, :, None]
    payload = whiten(spectra.astype(jnp.float32) * flag_values)
    row_index = lax.axis_index("row")
    col_index = lax.axis_index("col")
    col_count = lax.axis_size("col")
    row_count = lax.axis_size("row")
    half_size = row_count * per_device
    cols_here = col_count * per_device
    slot = jnp.arange(half_size, dtype=jnp.int32)
    first = (slot // per_device * col_count + col_index) * per_device + slot % per_device
    second = row_index * cols_here + jnp.arange(cols_here, dtype=jnp.int32)
    keep = (first[:, None] <= second[None, :]).astype(jnp.float32)[:, :, None]
    pieces = []
    for band_index in range(spectra.shape[0]):
        first_rows = lax.all_gather(payload[band_index : band_index + 1], "row", axis=3, tiled=True)
        second_rows = lax.all_gather(
            payload[band_index : band_index + 1], "col", axis=3, tiled=True
        )
        prods = jnp.einsum(
            "wpif,wqjf->pqijf", first_rows[0], second_rows[0], preferred_element_type=jnp.float32
        )
        pieces.append(combine_parts(prods, keep))
    result = jnp.stack(pieces, axis=0)
    return result[:, :, None]


def solution(mesh):
    in_specs = (P("parts", None, None, ("row", "col"), None), P("parts", ("row", "col")))
    out_specs = P("parts", None, "col", None, "row", None)
    return jax.shard_map(
        on_device, mesh=mesh, in_specs=in_specs, out_specs=out_specs, check_vma=False
    )
```

profile of v0, /device:TPU:0, one launch (start us, length us, event | category | flops | bytes accessed | tf_op | source)
XLA Modules:
  0.0 214.1 jit_solution(13793272223604262475)
XLA Ops:
  6.5 0.7 convert_element_type.26
  7.2 1.3 convert_multiply_fusion
  9.2 36.3 %reduce-window.6 = f32[2,32,2,10,128]{4,3,2,1,0:T(8,128)S(1)} reduce-window(f32[2,32,2,10,128]{4,3,2,1,0:T(8,128)S(1)} %copy.41, f32[]{:T(128)} %constant.44.clone.1), window={size=1x1x1x1x128 pad=0_0x0_0x0_0x0_0x127_0}, to_apply=%region_0.1 | reduce-window | flops 20807680 | bytes 1310724 | tf_op jit(solution)/shard_map/reduce-window
  45.8 0.5 copy.42
  47.1 0.6 fusion.37
  47.8 0.6 divide_convert_fusion
  48.3 0.8 fusion.38
  49.2 0.7 all-gather.3.cloned.1.call-update
  49.9 2.5 %all_gather.14 = bf16[1,32,2,4,1024]{4,1,2,0,3:T(8,128)(2,1)S(1)} all-gather(bf16[1,32,2,2,1024]{4,1,2,0,3:T(8,128)(2,1)} %get-tuple-element.12), channel_id=1, replica_groups=mesh['parts'=2,'row'=8,'col'=2] {'col'}, dimensions={3}, use_global_device_ids=true | all-gather | bytes 786432 | tf_op jit(solution)/shard_map/all_gather | solution.py:52
  52.5 2.6 %copy.52 = bf16[1,32,2,4,1024]{1,3,2,4,0:T(4,128)(2,1)} copy(bf16[1,32,2,4,1024]{4,1,2,0,3:T(8,128)(2,1)S(1)} %all_gather.14) | data formatting | bytes 1048576 | tf_op jit(solution)/shard_map/all_gather | solution.py:52
  55.0 2.4 %all_gather.12 = bf16[1,32,2,4,1024]{4,1,2,0,3:T(8,128)(2,1)S(1)} all-gather(bf16[1,32,2,2,1024]{4,1,2,0,3:T(8,128)(2,1)S(1)} %copy-done), channel_id=1, replica_groups=mesh['parts'=2,'row'=8,'col'=2] {'col'}, dimensions={3}, use_global_device_ids=true | all-gather | bytes 786432 | tf_op jit(solution)/shard_map/all_gather | solution.py:52
  57.4 1.4 copy.46
  58.9 42.3 %all-gather.5.cloned.1.call-done = bf16[1,32,2,16,1024]{4,1,2,0,3:T(8,128)(2,1)} async-done(((bf16[1,32,2,2,1024]{4,1,2,0,3:T(8,128)(2,1)}), bf16[1,32,2,16,1024]{4,1,2,0,3:T(8,128)(2,1)}) %all-gather.5.cloned.1.call-update) | async-done | bytes 2097168 | tf_op jit(solution)/shard_map/all_gather | solution.py:51
  101.1 12.5 %copy.53 = bf16[1,32,2,16,1024]{1,3,2,4,0:T(8,128)(2,1)} copy(bf16[1,32,2,16,1024]{4,1,2,0,3:T(8,128)(2,1)} %all-gather.5.cloned.1.call-done) | data formatting | bytes 4194304 | tf_op jit(solution)/shard_map/all_gather | solution.py:51
  113.6 26.9 %fusion.7 = f32[2,2,16,4,1024]{2,3,4,1,0:T(4,128)} fusion(bf16[1,32,2,16,1024]{1,3,2,4,0:T(8,128)(2,1)} %copy.53, bf16[1,32,2,4,1024]{1,3,2,4,0:T(4,128)(2,1)} %copy.52), kind=kOutput, calls=%fused_computation.5 | convolution fusion | flops 16777216 | bytes 3670016 | tf_op jit(solution)/shard_map/wpif,wqjf->pqijf/dot_general | solution.py:55
  140.5 10.4 %all-gather.3.cloned.1.call-done = bf16[1,32,2,16,1024]{4,1,2,0,3:T(8,128)(2,1)} async-done(((bf16[1,32,2,2,1024]{4,1,2,0,3:T(8,128)(2,1)}), bf16[1,32,2,16,1024]{4,1,2,0,3:T(8,128)(2,1)}) %all-gather.3.cloned.1.call-update) | async-done | bytes 2097168 | tf_op jit(solution)/shard_map/all_gather | solution.py:51
  150.9 12.5 %copy.47 = bf16[1,32,2,16,1024]{1,3,2,4,0:T(8,128)(2,1)} copy(bf16[1,32,2,16,1024]{4,1,2,0,3:T(8,128)(2,1)} %all-gather.3.cloned.1.call-done) | data formatting | bytes 4194304 | tf_op jit(solution)/shard_map/all_gather | solution.py:51
  163.4 26.2 %fusion.4 = f32[2,2,16,4,1024]{2,3,0,1,4:T(4,128)} fusion(bf16[1,32,2,16,1024]{1,3,2,4,0:T(8,128)(2,1)} %copy.47, bf16[1,32,2,4,1024]{1,3,2,4,0:T(4,128)(2,1)S(1)} %copy.46), kind=kOutput, calls=%fused_computation.4 | convolution fusion | flops 16777216 | bytes 3670016 | tf_op jit(solution)/shard_map/wpif,wqjf->pqijf/dot_general | solution.py:55
  189.7 9.5 %fusion.18 = (f32[1,16,4,1024]{1,2,3,0:T(4,128)}, f32[1,16,4,1024]{1,2,3,0:T(4,128)}, f32[1,16,4,1024]{1,2,3,0:T(4,128)S(1)}, f32[1,16,4,1024]{1,2,3,0:T(4,128)}) fusion(f32[2,2,16,4,1024]{2,3,0,1,4:T(4,128)} %fusion.4, f32[16,4]{0,1:T(4,128)S(1)} %compare_convert_fusion, f32[2,2,16,4,1024]{2,3,4,1,0:T(4,128)} %fusion.7), kind=kLoop, calls=%fused_computation.18 | loop fusion | flops 524288 | bytes 3145984 | tf_op jit(solution)/shard_map/mul | solution.py:32
  199.1 1.8 copy.50
  201.0 1.8 copy.51
  202.8 1.8 copy.55
  204.7 0.8 copy.56
  205.6 1.6 copy.57
  (23 shorter events, 2.2 us)
Async XLA Ops:
  6.5 94.6 %all-gather.5.cloned.1.call-start = ((), (), s32[]{:S(2)}) async-start(), calls=%async_computation.1 | async-start | bytes 2359296 | tf_op jit(solution)/shard_map/all_gather | solution.py:51
  46.7 1.0 copy-start.1
  49.2 5.9 %copy-start = (bf16[1,32,2,2,1024]{4,1,2,0,3:T(8,128)(2,1)S(1)}, bf16[1,32,2,2,1024]{4,1,2,0,3:T(8,128)(2,1)}, u32[]{:S(2)}) copy-start(bf16[1,32,2,2,1024]{4,1,2,0,3:T(8,128)(2,1)} %get-tuple-element.11) | copy-start | bytes 786436
  49.2 101.7 %all-gather.3.cloned.1.call-start = ((), (), s32[]{:S(2)}) async-start(), calls=%async_computation | async-start | bytes 2359296 | tf_op jit(solution)/shard_map/all_gather | solution.py:51
Sparse Core Ops, SparseCore 0:
  49.3 51.7 all-gather.4
  103.3 47.6 all-gather.2
where the time goes:
time: 214 us
  waiting for transfers between devices  53.4 us (25%)
  matrix products  53.1 us (25%)
  other arithmetic  49 us (23%)
  local copies, waits for them, and re-layouts  40.1 us (19%)
  between operations  13.5 us (6%)
  blocking collectives  4.86 us (2%)
    dot_general x2, matrix products, on_device(): jnp.einsum('wpif,wqjf->pqijf', first_rows[0], second_rows[0], preferred_e...  53.1 us
    all_gather x2, waiting for transfers between devices, on_device(): lax.all_gather(payload[band_index:band_index + 1], 'row', axis=3, tiled=T...  52.7 us
    another operation x3, other arithmetic  36.6 us
    all_gather x2, local copies, waits for them, and re-layouts, on_device(): lax.all_gather(payload[band_index:band_index + 1], 'row', axis=3, tiled=T...  25 us
    mul x1, other arithmetic, combine_parts(): return jnp.stack([real_part * keep, imag_part * keep], axis=-4)  9.47 us
    mul x4, local copies, waits for them, and re-layouts, combine_parts(): return jnp.stack([real_part * keep, imag_part * keep], axis=-4)  6.3 us
    all_gather x2, blocking collectives, on_device(): lax.all_gather(payload[band_index:band_index + 1], 'col', axis=3, tiled=T...  4.86 us
  transfers between devices with their start and end apart: 2, of which 2 were waited for; matrix products, arithmetic and copies ran while one was open for 20% of the time, Pallas kernels for 0%

commit v1 on v0

--- a/solution.py
+++ b/solution.py
@@ -5,6 +5,10 @@
 
 HALFWIN = 64
 epsilon = 1e-06
+update_the_targets = lambda u_in, link_axis, axis_k: jnp.concatenate(
+    jax.lax.all_to_all(jnp.stack(jax.lax.axis_size(link_axis) * [u_in], axis=0), link_axis, 0, 0),
+    axis_k,
+)
 
 
 def window_mean(magnitude):
@@ -48,7 +52,7 @@
     keep = (first[:, None] <= second[None, :]).astype(jnp.float32)[:, :, None]
     pieces = []
     for band_index in range(spectra.shape[0]):
-        first_rows = lax.all_gather(payload[band_index : band_index + 1], "row", axis=3, tiled=True)
+        first_rows = update_the_targets(payload[band_index : band_index + 1], "row", 3)
         second_rows = lax.all_gather(
             payload[band_index : band_index + 1], "col", axis=3, tiled=True
         )

time: 214 us -> 247 us (1.15); the launches traced: 214 us -> 244 us
  local copies, waits for them, and re-layouts: 40.1 us -> 57.6 us
  waiting for transfers between devices: 53.4 us -> 67.8 us
  between operations: 13.5 us -> 0.15 us
  starting transfers between devices: 0.04 us -> 11.6 us
    all_to_all x0 -> x2, waiting for transfers between devices: none -> 67.8 us  [jax.lax.all_to_all(jnp.stack(jax.lax.axis_size(link_axis) * [u_in], axis=...]
    all_gather x2 -> x0, waiting for transfers between devices: 52.7 us -> none  [on_device(): lax.all_gather(payload[band_index:band_index + 1], 'row', axis=3, tiled=T...]
    reshape x2 -> x4, local copies, waits for them, and re-layouts: 0.26 us -> 39.8 us  [the longest x2 39.5 us: jnp.concatenate(jax.lax.all_to_all(jnp.stack(jax.lax.axis_size(link_axis)...]
    all_gather x2 -> x0, local copies, waits for them, and re-layouts: 25 us -> none  [on_device(): lax.all_gather(payload[band_index:band_index + 1], 'row', axis=3, tiled=T...]
    all_to_all x0 -> x2, starting transfers between devices: none -> 11.6 us  [jax.lax.all_to_all(jnp.stack(jax.lax.axis_size(link_axis) * [u_in], axis=...]
    another operation x4 -> x6, local copies, waits for them, and re-layouts: 0.7 us -> 4.09 us  [the longest x2 3.39 us: jnp.stack(jax.lax.axis_size(link_axis) * [u_in], axis=0)]
  transfers between devices with their start and end apart: 2 -> 2, of which waited for: 2 -> 2; matrix products, arithmetic and copies ran while one was open for 20% -> 10% of each run, Pallas kernels for 0% -> 0%
where the time goes in v1:
time: 247 us; the launch traced here: 244 us
  waiting for transfers between devices  67.8 us (27%)
  local copies, waits for them, and re-layouts  57.6 us (23%)
  matrix products  53.3 us (22%)
  other arithmetic  49 us (20%)
  starting transfers between devices  11.6 us (5%)
  blocking collectives  4.36 us (2%)
    all_to_all x2, waiting for transfers between devices, jax.lax.all_to_all(jnp.stack(jax.lax.axis_size(link_axis) * [u_in], axis=...  67.8 us
    dot_general x2, matrix products, on_device(): jnp.einsum('wpif,wqjf->pqijf', first_rows[0], second_rows[0], preferred_e...  53.3 us
    reshape x2, local copies, waits for them, and re-layouts, jnp.concatenate(jax.lax.all_to_all(jnp.stack(jax.lax.axis_size(link_axis)...  39.5 us
    another operation x3, other arithmetic  36.6 us
    all_to_all x2, starting transfers between devices, jax.lax.all_to_all(jnp.stack(jax.lax.axis_size(link_axis) * [u_in], axis=...  11.6 us
    mul x1, other arithmetic, combine_parts(): return jnp.stack([real_part * keep, imag_part * keep], axis=-4)  9.48 us
    mul x4, local copies, waits for them, and re-layouts, combine_parts(): return jnp.stack([real_part * keep, imag_part * keep], axis=-4)  6.3 us
  transfers between devices with their start and end apart: 2, of which 2 were waited for; matrix products, arithmetic and copies ran while one was open for 10% of the time, Pallas kernels for 0%

profile of v1, /device:TPU:0, one launch (start us, length us, event | category | flops | bytes accessed | tf_op | source)
XLA Modules:
  0.0 243.9 jit_solution(17907882916548545751)
XLA Ops:
  0.0 0.7 convert_element_type.26
  0.7 1.3 convert_multiply_fusion
  2.6 36.3 %reduce-window.6 = f32[2,32,2,10,128]{4,3,2,1,0:T(8,128)S(1)} reduce-window(f32[2,32,2,10,128]{4,3,2,1,0:T(8,128)S(1)} %copy.43, f32[]{:T(128)} %constant.44.clone.1), window={size=1x1x1x1x128 pad=0_0x0_0x0_0x0_0x127_0}, to_apply=%region_0.1 | reduce-window | flops 20807680 | bytes 1310724 | tf_op jit(solution)/shard_map/reduce-window
  40.6 0.6 fusion.32
  42.0 1.6 stack.17
  43.5 7.3 %all-to-all-start.1 = ((bf16[8,1,32,2,2,1024]{5,2,4,3,1,0:T(8,128)(2,1)}), bf16[8,1,32,2,2,1024]{5,2,4,3,1,0:T(8,128)(2,1)S(1)}, u32[]{:S(2)}, u32[]{:S(2)}) async-start(bf16[8,1,32,2,2,1024]{5,2,4,3,1,0:T(8,128)(2,1)} %stack.17), calls=%async_computation.1 | async-start | bytes 4194304 | tf_op jit(solution)/shard_map/all_to_all | solution.py:9
  50.9 48.2 %all-to-all-done.1 = bf16[8,1,32,2,2,1024]{5,2,4,3,1,0:T(8,128)(2,1)S(1)} async-done(((bf16[8,1,32,2,2,1024]{5,2,4,3,1,0:T(8,128)(2,1)}), bf16[8,1,32,2,2,1024]{5,2,4,3,1,0:T(8,128)(2,1)S(1)}, u32[]{:S(2)}, u32[]{:S(2)}) %all-to-all-start.1) | async-done | bytes 2097184 | tf_op jit(solution)/shard_map/all_to_all | solution.py:9
  99.1 1.8 stack.14
  101.1 4.3 %all-to-all-start = ((bf16[8,1,32,2,2,1024]{5,2,4,3,1,0:T(8,128)(2,1)}), bf16[8,1,32,2,2,1024]{5,2,4,3,1,0:T(8,128)(2,1)}, u32[]{:S(2)}, u32[]{:S(2)}) async-start(bf16[8,1,32,2,2,1024]{5,2,4,3,1,0:T(8,128)(2,1)} %stack.14), calls=%async_computation | async-start | bytes 4194304 | tf_op jit(solution)/shard_map/all_to_all | solution.py:9
  105.4 2.2 all_gather.7
  107.6 1.4 copy.55
  109.0 2.2 all_gather.6
  111.2 2.6 %copy.48 = bf16[1,32,2,4,1024]{1,3,2,4,0:T(4,128)(2,1)} copy(bf16[1,32,2,4,1024]{4,1,2,0,3:T(8,128)(2,1)S(1)} %all_gather.6) | data formatting | bytes 1048576 | tf_op jit(solution)/shard_map/all_gather | solution.py:56
  113.8 19.8 %copy.57 = bf16[1,32,2,8,2,1024]{1,4,3,2,5,0:T(2,128)(2,1)} copy(bf16[1,32,2,8,2,1024]{5,1,4,2,0,3:T(8,128)(2,1)} %bitcast.75) | data formatting | bytes 4194304 | tf_op jit(solution)/shard_map/reshape | solution.py:8
  133.6 19.6 %all-to-all-done = bf16[8,1,32,2,2,1024]{5,2,4,3,1,0:T(8,128)(2,1)} async-done(((bf16[8,1,32,2,2,1024]{5,2,4,3,1,0:T(8,128)(2,1)}), bf16[8,1,32,2,2,1024]{5,2,4,3,1,0:T(8,128)(2,1)}, u32[]{:S(2)}, u32[]{:S(2)}) %all-to-all-start) | async-done | bytes 2097184 | tf_op jit(solution)/shard_map/all_to_all | solution.py:9
  153.2 19.7 %copy.50 = bf16[1,32,2,8,2,1024]{1,4,3,2,5,0:T(2,128)(2,1)} copy(bf16[1,32,2,8,2,1024]{5,1,4,2,0,3:T(8,128)(2,1)} %bitcast.6) | data formatting | bytes 4194304 | tf_op jit(solution)/shard_map/reshape | solution.py:8
  173.0 26.2 %fusion.2 = f32[2,2,16,4,1024]{2,3,4,1,0:T(4,128)} fusion(bf16[32,2,16,1024,1]{0,2,1,3,4:T(8,128)(2,1)} %bitcast.73, bf16[1,32,2,4,1024]{1,3,2,4,0:T(4,128)(2,1)S(1)} %copy.55), kind=kOutput, calls=%fused_computation.3 | convolution fusion | flops 16777216 | bytes 3670016 | tf_op jit(solution)/shard_map/wpif,wqjf->pqijf/dot_general | solution.py:59
  199.2 27.1 %convolution_bitcast_fusion = f32[2,2,16,4,1024]{2,3,0,1,4:T(4,128)} fusion(bf16[32,2,16,1024,1]{0,2,1,4,3:T(8,128)(2,1)} %bitcast.74, bf16[1,32,2,4,1024]{1,3,2,4,0:T(4,128)(2,1)} %copy.48), kind=kOutput, calls=%fused_computation.2 | convolution fusion | flops 16777216 | bytes 3670016 | tf_op jit(solution)/shard_map/wpif,wqjf->pqijf/dot_general | solution.py:59
  226.3 9.5 %fusion.13 = (f32[1,16,4,1024]{1,2,3,0:T(4,128)}, f32[1,16,4,1024]{1,2,3,0:T(4,128)}, f32[1,16,4,1024]{1,2,3,0:T(4,128)S(1)}, f32[1,16,4,1024]{1,2,3,0:T(4,128)}) fusion(f32[2,2,16,4,1024]{2,3,0,1,4:T(4,128)} %convolution_bitcast_fusion, f32[16,4]{0,1:T(4,128)S(1)} %compare_convert_fusion, f32[2,2,16,4,1024]{2,3,4,1,0:T(4,128)} %fusion.2), kind=kLoop, calls=%fused_computation.16 | loop fusion | flops 524288 | bytes 3145984 | tf_op jit(solution)/shard_map/mul | solution.py:36
  235.7 1.8 copy.53
  237.6 1.8 copy.54
  239.4 1.8 copy.59
  241.3 0.8 copy.60
  242.2 1.6 copy.61
  (25 shorter events, 3.5 us)
Async XLA Ops:
  40.2 1.0 copy-start.1
  43.5 55.5 %all-to-all-start.1 = ((bf16[8,1,32,2,2,1024]{5,2,4,3,1,0:T(8,128)(2,1)}), bf16[8,1,32,2,2,1024]{5,2,4,3,1,0:T(8,128)(2,1)S(1)}, u32[]{:S(2)}, u32[]{:S(2)}) async-start(bf16[8,1,32,2,2,1024]{5,2,4,3,1,0:T(8,128)(2,1)} %stack.17), calls=%async_computation.1 | async-start | bytes 4194304 | tf_op jit(solution)/shard_map/all_to_all | solution.py:9
  99.1 2.0 copy-start
  101.1 52.2 %all-to-all-start = ((bf16[8,1,32,2,2,1024]{5,2,4,3,1,0:T(8,128)(2,1)}), bf16[8,1,32,2,2,1024]{5,2,4,3,1,0:T(8,128)(2,1)}, u32[]{:S(2)}, u32[]{:S(2)}) async-start(bf16[8,1,32,2,2,1024]{5,2,4,3,1,0:T(8,128)(2,1)} %stack.14), calls=%async_computation | async-start | bytes 4194304 | tf_op jit(solution)/shard_map/all_to_all | solution.py:9
